TPU v7x, 512 devices: a whole 4x4x16 slice. The times are simulated.
512 devices in a mesh: req: 64 (over z, y), tensor: 8 (over x, core).
Axes of the slice: x: 4, y: 4, z: 16, core: 2. Of those that a mesh axis runs over, the one named last changes fastest.
Arguments:
- tokens: bfloat16 [16384, 2048], P('req', 'tensor'), may hold values from -6 to 6
- segment_ids: int32 [16384], P('req'), may hold values from 0 to 42, as said below
- prefix_lengths: int32 [43], replicated, may hold values from 0 to 256, as said below
- page_owner: int32 [4096, 1], P('req'), may hold values from 0 to 63; in each aligned block of 64 rows (0 to 63, 64 to 127, ...) at most 2 rows name the same one
- slot_perm: int32 [64, 128], P('req'), may hold values from 0 to 127, each once within a row
- ln_gain: float32 [2048], replicated, may hold values from 0.1 to 1.9
- ln_bias: float32 [2048], replicated, may hold values from -3 to 3
- qkv_weight: bfloat16 [2048, 3, 2048], P('req', None, 'tensor')
- qkv_bias: float32 [3, 2048], P(None, 'tensor'), may hold values from -3 to 3
- dense_weight: bfloat16 [2048, 2048], P('tensor', 'req'), may hold values from -0.375 to 0.375
- dense_bias: float32 [2048], P('tensor'), may hold values from -3 to 3
- fc1_weight: bfloat16 [2048, 4096], P('req', 'tensor'), may hold values from -0.125 to 0.125
- fc1_bias: float32 [4096], P('tensor'), may hold values from -3 to 3
- fc2_weight: bfloat16 [4096, 2048], P('tensor', 'req'), may hold values from -0.25 to 0.25
- fc2_bias: float32 [2048], P('tensor'), may hold values from -3 to 3
- prefix_cache: bfloat16 [16384, 2, 2048], P('req', None, 'tensor'), may hold values from -9 to 9
- cache_pool: bfloat16 [32768, 2, 2048], P('req', None, 'tensor'), may hold values from -6 to 6
Outputs:
- layer_out: bfloat16 [16384, 2048], P('req', 'tensor')
- new_pool: bfloat16 [32768, 2, 2048], P('req', None, 'tensor')
Inputs may be any that keep to these rules, and one draw needn't show every extreme that they name: `segment_ids`: labels 1 to 42 appear in order, each as one run of 257 to 512 rows, together filling all rows before the padding; segment 1 is 512 rows long; the last 128 rows are 0. `prefix_lengths`: entry 0 is 0 and entry 1 is 256. `page_owner`: among the pages of one index of req no owner appears more than 2 times, and some owner appears exactly 2 times. `slot_perm`: each row is a permutation of 0 to 127.
All inputs are finite; a program needn't handle non-finite values.
Results may differ from a plain program's by a relative error of at most 0.006.
The roundings to bfloat16 on the way count: a program that leaves them out, or rounds other values in their place, can miss the bound.
Values may be sent and summed in bfloat16 or wider, within the bound.
A program may use at most 64 MiB of HBM per device.

v0:
```python
import jax
import jax.numpy as jnp
from jax import lax
from jax.sharding import PartitionSpec as P

HEAD_DIM = 64
ROT = 32
SPAN = 2
SINKS = 4
PAGE = 4
WINDOW = 512
EPSILON = 1e-05


def from_behind(value, axis, steps):
    count = lax.axis_size(axis)
    leading, last = (max(0, -steps), min(count, count - steps))
    return lax.ppermute(value, axis, [(source, source + steps) for source in range(leading, last)])


def norm_rows(widened, gain, offset_bias):
    average = jnp.mean(widened, axis=-1, keepdims=True)
    centred = widened - average
    spread = jnp.mean(centred * centred, axis=-1, keepdims=True)
    return (centred * lax.rsqrt(spread + EPSILON) * gain + offset_bias).astype(jnp.bfloat16)


def label_rows(places, starts, prefix_lengths):
    labels = jnp.arange(starts.shape[0], dtype=jnp.int32)
    passed = (starts[None, :] <= places[:, None]) & (labels[None, :] >= 1)
    counted = jnp.sum(passed.astype(jnp.int32), axis=1)
    segment = jnp.where(places >= starts[0], 0, counted)
    segment = jnp.where(places < 0, -2, segment)
    onehot = segment[:, None] == labels[None, :]
    earliest = jnp.sum(jnp.where(onehot, starts[None, :], 0), axis=1)
    offset = jnp.sum(jnp.where(onehot, prefix_lengths[None, :], 0), axis=1)
    return (segment, offset + places - earliest)


def prefix_rows(block_id, rows_dev, prefix_count, starts, prefix_lengths):
    labels = jnp.arange(starts.shape[0], dtype=jnp.int32)
    located = (starts >= block_id * rows_dev) & (starts < (block_id + 1) * rows_dev) & (labels >= 1)
    owner_label = jnp.sum(jnp.where(located, labels, 0))
    length = jnp.sum(jnp.where(located, prefix_lengths, 0))
    places = jnp.arange(prefix_count, dtype=jnp.int32)
    usable = jnp.any(located) & (places < length)
    return (jnp.where(usable, owner_label, -2), places)


def rotate_heads(values, position):
    half_rot = ROT // 2
    frequency = 10000.0 ** (-2.0 * jnp.arange(half_rot, dtype=jnp.float32) / ROT)
    angles = position.astype(jnp.float32)[:, None] * frequency[None, :]
    cosine = jnp.cos(angles)[:, None, :]
    sine_vals = jnp.sin(angles)[:, None, :]
    lower = values[..., :half_rot]
    upper = values[..., half_rot:ROT]
    return jnp.concatenate(
        [lower * cosine - upper * sine_vals, upper * cosine + lower * sine_vals, values[..., ROT:]],
        axis=-1,
    )


def head_attention(query_rows, key_rows, value_rows, allowed):
    head_count = query_rows.shape[1] // HEAD_DIM
    score_scale = HEAD_DIM ** (-0.5)

    def one_head(head_index):
        query_cols = lax.dynamic_slice_in_dim(query_rows, head_index * HEAD_DIM, HEAD_DIM, 1)
        key_cols = lax.dynamic_slice_in_dim(key_rows, head_index * HEAD_DIM, HEAD_DIM, 1)
        value_cols = lax.dynamic_slice_in_dim(value_rows, head_index * HEAD_DIM, HEAD_DIM, 1)
        scores = (
            lax.dot_general(
                query_cols, key_cols, (((1,), (1,)), ((), ())), preferred_element_type=jnp.float32
            )
            * score_scale
        )
        masked = jnp.where(allowed, scores, -1e30)
        highest = jnp.max(masked, axis=1, keepdims=True)
        expo = jnp.where(allowed, jnp.exp(masked - highest), 0.0)
        denom = jnp.sum(expo, axis=1, keepdims=True)
        mixed = (
            jnp.dot(expo.astype(jnp.bfloat16), value_cols, preferred_element_type=jnp.float32)
            / denom
        )
        return mixed.astype(jnp.bfloat16)

    outcome = lax.map(one_head, jnp.arange(head_count, dtype=jnp.int32))
    return jnp.transpose(outcome, (1, 0, 2)).reshape(query_rows.shape[0], head_count * HEAD_DIM)


def shards(
    tokens,
    segment_ids,
    prefix_lengths,
    page_owner,
    slot_perm,
    ln_gain,
    ln_bias,
    qkv_weight,
    qkv_bias,
    dense_weight,
    dense_bias,
    fc1_weight,
    fc1_bias,
    fc2_weight,
    fc2_bias,
    prefix_cache,
    cache_pool,
):
    req_count = lax.axis_size("req")
    req_index = lax.axis_index("req")
    tok_rows = tokens.shape[0]
    prefix_count = prefix_cache.shape[0]
    head_cols = qkv_weight.shape[2]
    pool_count = slot_perm.shape[1]
    page_cap = pool_count // req_count
    gathered = lax.all_gather(tokens, "tensor", axis=1, tiled=True)
    normed = norm_rows(gathered.astype(jnp.float32), ln_gain, ln_bias)
    row_ids = jnp.arange(tok_rows, dtype=jnp.int32)
    places = req_index * tok_rows + row_ids
    labels = jnp.arange(prefix_lengths.shape[0], dtype=jnp.int32)
    beyond = tok_rows * req_count
    earliest_rows = jnp.min(
        jnp.where(segment_ids[:, None] == labels[None, :], places[:, None], beyond), axis=0
    )
    starts = lax.pmin(earliest_rows, "req")

    def add_rows(portion):
        return jnp.dot(normed, portion, preferred_element_type=jnp.float32)

    qkv_local = qkv_weight.reshape(qkv_weight.shape[0], 3 * head_cols)
    projected = add_rows(lax.all_gather(qkv_local, "req", axis=0, tiled=True))
    lifted = add_rows(lax.all_gather(fc1_weight, "req", axis=0, tiled=True))
    projected = (projected + qkv_bias.reshape(1, 3 * head_cols)).reshape(
        tok_rows, 3, head_cols // HEAD_DIM, HEAD_DIM
    )
    segment, position = label_rows(places, starts, prefix_lengths)
    queries = (
        rotate_heads(projected[:, 0], position).astype(jnp.bfloat16).reshape(tok_rows, head_cols)
    )
    new_keys = (
        rotate_heads(projected[:, 1], position).astype(jnp.bfloat16).reshape(tok_rows, head_cols)
    )
    new_values = projected[:, 2].astype(jnp.bfloat16).reshape(tok_rows, head_cols)
    key_value = jnp.stack([new_keys, new_values], axis=1)
    pages_here = tok_rows // PAGE
    pages = key_value.reshape(pages_here, PAGE * 2 * head_cols)
    owners = page_owner[:, 0]
    onehot = (owners[:, None] == jnp.arange(req_count, dtype=jnp.int32)[None, :]).astype(jnp.int32)
    earlier = jnp.cumsum(onehot, axis=0) - onehot
    earlier_count = jnp.sum(earlier * onehot, axis=1)
    target = owners * page_cap + earlier_count
    selecting = (target[None, :] == jnp.arange(pool_count, dtype=jnp.int32)[:, None]).astype(
        jnp.bfloat16
    )
    outgoing = jnp.dot(selecting, pages, preferred_element_type=jnp.float32).astype(jnp.bfloat16)
    filled = jnp.sum(selecting, axis=1)
    incoming, incoming_filled = (
        lax.all_to_all(
            outgoing.reshape(req_count, page_cap, PAGE * 2 * head_cols),
            "req",
            split_axis=0,
            concat_axis=0,
            tiled=True,
        ),
        lax.all_to_all(
            filled.reshape(req_count, page_cap), "req", split_axis=0, concat_axis=0, tiled=True
        ),
    )
    slot_ids = slot_perm[0]
    placing = (slot_ids[None, :] == jnp.arange(pool_count, dtype=jnp.int32)[:, None]) & (
        incoming_filled.reshape(pool_count)[None, :] > 0
    )
    written = jnp.dot(
        placing.astype(jnp.bfloat16),
        incoming.reshape(pool_count, PAGE * 2 * head_cols),
        preferred_element_type=jnp.float32,
    ).astype(jnp.bfloat16)
    written_mask = jnp.any(placing, axis=1)
    pool_pages = cache_pool.reshape(pool_count, PAGE * 2 * head_cols)
    new_pool = jnp.where(written_mask[:, None], written, pool_pages).reshape(cache_pool.shape)
    local_keys = jnp.concatenate([key_value, prefix_cache], axis=0)
    blocks = [local_keys]
    for shift_by in range(1, SPAN + 1):
        blocks.append(from_behind(local_keys, "req", shift_by))
    key_segs = []
    key_poss = []
    for step_back in range(SPAN + 1):
        block_id = req_index - step_back
        seg_new, pos_new = label_rows(block_id * tok_rows + row_ids, starts, prefix_lengths)
        seg_old, pos_old = prefix_rows(block_id, tok_rows, prefix_count, starts, prefix_lengths)
        key_segs.extend([seg_new, seg_old])
        key_poss.extend([pos_new, pos_old])
    key_segment = jnp.concatenate(key_segs)
    key_position = jnp.concatenate(key_poss)
    allowed = (key_segment[None, :] == segment[:, None]) & (
        key_position[None, :] <= position[:, None]
    )
    allowed = allowed & (
        (position[:, None] - key_position[None, :] < WINDOW) | (key_position[None, :] < SINKS)
    )
    all_keys = jnp.concatenate(blocks, axis=0)
    attended = head_attention(queries, all_keys[:, 0, :], all_keys[:, 1, :], allowed)
    hidden = jax.nn.gelu(lifted + fc1_bias, approximate=True).astype(jnp.bfloat16)
    attn_part = jnp.dot(
        attended,
        lax.all_gather(dense_weight, "req", axis=1, tiled=True),
        preferred_element_type=jnp.float32,
    )
    mlp_part = jnp.dot(
        hidden,
        lax.all_gather(fc2_weight, "req", axis=1, tiled=True),
        preferred_element_type=jnp.float32,
    )
    branches = attn_part + mlp_part
    summed = lax.psum_scatter(branches, "tensor", scatter_dimension=1, tiled=True)
    layer_out = (tokens.astype(jnp.float32) + summed + dense_bias + fc2_bias).astype(jnp.bfloat16)
    return (layer_out, new_pool)


def solution(mesh):
    placed = (
        P("req", "tensor"),
        P("req"),
        P(),
        P("req", None),
        P("req", None),
        P(),
        P(),
        P("req", None, "tensor"),
        P(None, "tensor"),
        P("tensor", "req"),
        P("tensor"),
        P("req", "tensor"),
        P("tensor"),
        P("tensor", "req"),
        P("tensor"),
        P("req", None, "tensor"),
        P("req", None, "tensor"),
    )
    return jax.shard_map(
        shards,
        mesh=mesh,
        in_specs=placed,
        out_specs=(P("req", "tensor"), P("req", None, "tensor")),
        check_vma=False,
    )
```

profile of v0, /device:TPU:2, one launch (start us, length us, event | category | flops | bytes accessed | tf_op | source)
XLA Modules:
  0.0 680.2 jit_solution(15321426984740319894)
XLA Ops:
  12.2 34.2 %pmin.7 = s32[43]{0:T(128)S(1)} all-reduce(s32[43]{0:T(128)S(1)} %select_reduce_fusion.6), channel_id=1, replica_groups=mesh['req'=64,'tensor'=8] {'req'}, use_global_device_ids=true, to_apply=%region_3.4 | all-reduce | flops 43 | bytes 344 | tf_op jit(solution)/shard_map/pmin | solution.py:127
  47.1 1.4 select_reduce_fusion.9
  49.4 1.9 constant_dynamic-update-slice_fusion.8
  51.3 1.9 constant_dynamic-update-slice_fusion.4
  56.2 1.5 convert_reduce_fusion
  57.7 1.6 fusion.23
  59.4 134.8 %all-gather.8.cloned.1.call-done = bf16[2048,768]{1,0:T(8,128)(2,1)} async-done(((bf16[32,768]{1,0:T(8,128)(2,1)}), bf16[2048,768]{1,0:T(8,128)(2,1)}) %all-gather.8.cloned.1.call-update) | async-done | bytes 3145744 | tf_op jit(solution)/shard_map/all_gather | solution.py:133
  194.2 3.0 convolution_add_fusion.1
  197.7 1.9 collective-permute-start
  199.6 4.1 collective-permute-start.1
  203.7 1.9 constant_dynamic-update-slice_fusion
  205.7 2.8 collective-permute-done
  208.5 5.8 collective-permute-done.1
  214.5 15.9 %while.11 = (s32[]{:T(128)}, bf16[4,256,64]{1,2,0:T(8,128)(2,1)S(1)}, s32[4]{0:T(128)S(1)}, bf16[256,256]{0,1:T(8,128)(2,1)S(1)}, bf16[1536,256]{0,1:T(8,128)(2,...) while((s32[]{:T(128)}, ...), condition=%wide.region_25.26_spmd.clone, body=%wide.region_22.25_spmd.clone.sunk | while | flops 112492032 | bytes 5240527 | solution.py:88
  230.4 100.3 %all-gather.10.cloned.1.call-done = bf16[256,2048]{0,1:T(8,128)(2,1)} async-done(((bf16[256,32]{0,1:T(8,128)(2,1)}), bf16[256,2048]{0,1:T(8,128)(2,1)}) %all-gather.10.cloned.1.call-update) | async-done | bytes 1048592 | tf_op jit(solution)/shard_map/all_gather | solution.py:208
  330.7 1.7 fusion.59
  332.5 138.2 %all-gather.12.cloned.1.call-done = bf16[2048,512]{1,0:T(8,128)(2,1)} async-done(((bf16[32,512]{1,0:T(8,128)(2,1)}), bf16[2048,512]{1,0:T(8,128)(2,1)}) %all-gather.12.cloned.1.call-update) | async-done | bytes 2097168 | tf_op jit(solution)/shard_map/all_gather | solution.py:134
  470.7 139.8 %all-gather.14.cloned.1.call-done = bf16[512,2048]{0,1:T(8,128)(2,1)} async-done(((bf16[512,32]{0,1:T(8,128)(2,1)}), bf16[512,2048]{0,1:T(8,128)(2,1)}) %all-gather.14.cloned.1.call-update) | async-done | bytes 2097168 | tf_op jit(solution)/shard_map/all_gather | solution.py:213
  610.5 5.1 convolution_add_fusion
  617.5 10.3 %all-to-all-start = ((bf16[64,1,2]{2,1,0:T(2,128)(2,1)}), bf16[64,1,2]{2,1,0:T(2,128)(2,1)S(1)}, u32[]{:S(2)}, u32[]{:S(2)}) async-start(bf16[64,1,2]{2,1,0:T(2,128)(2,1)} %all_to_all.12), calls=%async_computation.1 | async-start | bytes 65536 | tf_op jit(solution)/shard_map/all_to_all | solution.py:167
  629.7 12.6 %all-to-all-done = bf16[64,1,2]{2,1,0:T(2,128)(2,1)S(1)} async-done(((bf16[64,1,2]{2,1,0:T(2,128)(2,1)}), bf16[64,1,2]{2,1,0:T(2,128)(2,1)S(1)}, u32[]{:S(2)}, u32[]{:S(2)}) %all-to-all-start) | async-done | bytes 288 | tf_op jit(solution)/shard_map/all_to_all | solution.py:167
  642.4 4.6 all-to-all-start.1
  647.8 22.2 %all-to-all-done.1 = bf16[64,2,2048]{2,1,0:T(2,128)(2,1)S(1)} async-done(((bf16[64,2,2048]{2,1,0:T(2,128)(2,1)}), bf16[64,2,2048]{2,1,0:T(2,128)(2,1)S(1)}, u32[]{:S(2)}, u32[]{:S(2)}) %all-to-all-start.1) | async-done | bytes 524320 | tf_op jit(solution)/shard_map/all_to_all | solution.py:160
  671.7 1.7 add_convert_fusion
  (109 shorter events, 29.5 us)
Async XLA Ops:
  7.2 187.0 %copy-start.9 = (f32[2048]{0:T(1024)S(1)}, f32[2048]{0:T(1024)}, u32[]{:S(2)}) copy-start(f32[2048]{0:T(1024)} %param.24) | copy-start | bytes 24580
  7.2 187.0 %copy-start.7 = (f32[2048]{0:T(1024)S(1)}, f32[2048]{0:T(1024)}, u32[]{:S(2)}) copy-start(f32[2048]{0:T(1024)} %param.25) | copy-start | bytes 24580
  7.2 49.0 %all-gather.6.cloned.1.call-start = ((), (), s32[]{:S(2)}) async-start(), calls=%async_computation.3 | async-start | bytes 1179648 | tf_op jit(solution)/shard_map/all_gather | solution.py:118
  7.9 186.3 %all-gather.8.cloned.1.call-start = ((), (), s32[]{:S(2)}) async-start(), calls=%async_computation.4 | async-start | bytes 3194880 | tf_op jit(solution)/shard_map/all_gather | solution.py:133
  9.4 321.3 %all-gather.10.cloned.1.call-start = ((), (), s32[]{:S(2)}) async-start(), calls=%async_computation.5 | async-start | bytes 1064960 | tf_op jit(solution)/shard_map/all_gather | solution.py:208
  10.2 460.5 %all-gather.12.cloned.1.call-start = ((), (), s32[]{:S(2)}) async-start(), calls=%async_computation.6 | async-start | bytes 2129920 | tf_op jit(solution)/shard_map/all_gather | solution.py:134
  10.7 599.7 %all-gather.14.cloned.1.call-start = ((), (), s32[]{:S(2)}) async-start(), calls=%async_computation.7 | async-start | bytes 2129920 | tf_op jit(solution)/shard_map/all_gather | solution.py:213
  11.3 660.4 %reduce-scatter.2.cloned.1.call-start = ((), (), s32[]{:S(2)}) async-start(), calls=%async_computation.8 | async-start | bytes 2359296 | tf_op jit(solution)/shard_map/reduce_scatter | solution.py:217
  56.1 138.1 %copy-start = (bf16[256,2048]{1,0:T(8,128)(2,1)S(1)}, bf16[256,2048]{1,0:T(8,128)(2,1)}, u32[]{:S(2)}) copy-start(bf16[256,2048]{1,0:T(8,128)(2,1)} %all-gather.6.cloned.1.call-done) | copy-start | bytes 3145732
  197.7 10.8 %collective-permute-start = (bf16[512,2,256]{0,2,1:T(8,128)(2,1)S(1)}, bf16[512,2,256]{0,2,1:T(8,128)(2,1)S(1)}, u32[]{:S(2)}, u32[]{:S(2)}) collective-permute-start(bf16[512,2,256]{0,2,1:T(8,128)(2,1)S(1)} %pad_maximum_fusion.1), channel_id=1, source_target_pairs={{0,8},{8,16},{16,24},{24,32},{32,40},{40,48},{48,56},{56,64},{64,7... | collective-permute-start | bytes 1572872 | tf_op jit(solution)/shard_map/ppermute | solution.py:18
  199.6 14.6 %collective-permute-start.1 = (bf16[512,2,256]{0,2,1:T(8,128)(2,1)S(1)}, bf16[512,2,256]{0,2,1:T(8,128)(2,1)S(1)}, u32[]{:S(2)}, u32[]{:S(2)}) collective-permute-start(bf16[512,2,256]{0,2,1:T(8,128)(2,1)S(1)} %pad_maximum_fusion.1), channel_id=1, source_target_pairs={{0,16},{8,24},{16,32},{24,40},{32,48},{40,56},{48,64},{56,72},{64,... | collective-permute-start | bytes 1572872 | tf_op jit(solution)/shard_map/ppermute | solution.py:18
  230.4 380.0 %copy-start.8 = (f32[2048]{0:T(1024)S(1)}, f32[2048]{0:T(1024)}, u32[]{:S(2)}) copy-start(f32[2048]{0:T(1024)} %param.25) | copy-start | bytes 24580
  615.6 0.7 copy-start.3
  617.5 24.9 %all-to-all-start = ((bf16[64,1,2]{2,1,0:T(2,128)(2,1)}), bf16[64,1,2]{2,1,0:T(2,128)(2,1)S(1)}, u32[]{:S(2)}, u32[]{:S(2)}) async-start(bf16[64,1,2]{2,1,0:T(2,128)(2,1)} %all_to_all.12), calls=%async_computation.1 | async-start | bytes 65536 | tf_op jit(solution)/shard_map/all_to_all | solution.py:167
  627.8 19.2 %copy-start.1 = (bf16[512,2,256]{2,1,0:T(2,128)(2,1)S(1)}, bf16[512,2,256]{2,1,0:T(2,128)(2,1)}, u32[]{:S(2)}) copy-start(bf16[512,2,256]{2,1,0:T(2,128)(2,1)} %param.35) | copy-start | bytes 1572868
  628.2 19.5 %copy-start.6 = (s32[1,128]{1,0:T(1,128)S(1)}, s32[1,128]{1,0:T(1,128)}, u32[]{:S(2)}) copy-start(s32[1,128]{1,0:T(1,128)} %param.23) | copy-start | bytes 1540
  642.4 27.6 %all-to-all-start.1 = ((bf16[64,2,2048]{2,1,0:T(2,128)(2,1)}), bf16[64,2,2048]{2,1,0:T(2,128)(2,1)S(1)}, u32[]{:S(2)}, u32[]{:S(2)}) async-start(bf16[64,2,2048]{2,1,0:T(2,128)(2,1)} %reshape.254), calls=%async_computation.2 | async-start | bytes 1048576 | tf_op jit(solution)/shard_map/all_to_all | solution.py:160
  647.4 24.3 %copy-start.2 = (bf16[256,256]{1,0:T(8,128)(2,1)S(1)}, bf16[256,256]{1,0:T(8,128)(2,1)}, u32[]{:S(2)}) copy-start(bf16[256,256]{1,0:T(8,128)(2,1)} %param.19) | copy-start | bytes 393220
  647.4 24.3 %copy-start.4 = (f32[256]{0:T(256)S(1)}, f32[256]{0:T(256)}, u32[]{:S(2)}) copy-start(f32[256]{0:T(256)} %param.33) | copy-start | bytes 3076
  647.4 24.3 %copy-start.5 = (f32[256]{0:T(256)S(1)}, f32[256]{0:T(256)}, u32[]{:S(2)}) copy-start(f32[256]{0:T(256)} %param.29) | copy-start | bytes 3076
Sparse Core Ops, SparseCore 0:
  10.1 34.8 all-gather.5
  48.6 145.5 all-gather.7
  197.1 133.5 all-gather.9
  333.5 137.0 all-gather.11
  473.5 136.9 all-gather.13
  615.7 34.3 reduce-scatter.1
where the time goes:
time: 681 us; the launch traced here: 680 us
  waiting for transfers between devices  559 us (82%)
  blocking collectives  34.2 us (5%)
  starting transfers between devices  21.1 us (3%)
  other arithmetic  20 us (3%)
  matrix products  17.7 us (3%)
  between operations  14.6 us (2%)
  local copies, waits for them, and re-layouts  10.9 us (2%)
    all_gather x1, waiting for transfers between devices, shards(): lax.all_gather(fc2_weight, 'req', axis=1, tiled=True)  140 us
    all_gather x1, waiting for transfers between devices, shards(): lifted = add_rows(lax.all_gather(fc1_weight, 'req', axis=0, tiled=True))  138 us
    all_gather x1, waiting for transfers between devices, shards(): projected = add_rows(lax.all_gather(qkv_local, 'req', axis=0, tiled=True))  135 us
    all_gather x1, waiting for transfers between devices, shards(): lax.all_gather(dense_weight, 'req', axis=1, tiled=True)  100 us
    pmin x1, blocking collectives, shards(): starts = lax.pmin(earliest_rows, 'req')  34.2 us
    all_to_all x1, waiting for transfers between devices, shards(): lax.all_to_all(outgoing.reshape(req_count, page_cap, PAGE * 2 * head_cols...  22.2 us
  transfers between devices with their start and end apart: 10, of which 8 were waited for; matrix products, arithmetic and copies ran while one was open for 6% of the time, Pallas kernels for 0%

commit v1 on v0

--- a/solution.py
+++ b/solution.py
@@ -10,6 +10,13 @@
 PAGE = 4
 WINDOW = 512
 EPSILON = 1e-05
+
+
+def gather_over(block, name, dim):
+    size = lax.axis_size(name)
+    parts = jnp.stack([block for _ in range(size)])
+    parts = lax.all_to_all(parts, name, split_axis=0, concat_axis=0)
+    return jnp.concatenate(parts, axis=dim)
 
 
 def from_behind(value, axis, steps):
@@ -204,9 +211,7 @@
     attended = head_attention(queries, all_keys[:, 0, :], all_keys[:, 1, :], allowed)
     hidden = jax.nn.gelu(lifted + fc1_bias, approximate=True).astype(jnp.bfloat16)
     attn_part = jnp.dot(
-        attended,
-        lax.all_gather(dense_weight, "req", axis=1, tiled=True),
-        preferred_element_type=jnp.float32,
+        attended, gather_over(dense_weight, "req", 1), preferred_element_type=jnp.float32
     )
     mlp_part = jnp.dot(
         hidden,

time: 681 us -> 545 us (0.80)
  waiting for transfers between devices: 559 us -> 372 us
  blocking collectives: 34.2 us -> 61.2 us
  starting transfers between devices: 21.1 us -> 40.1 us
    all_gather x1 -> x0, waiting for transfers between devices: 100 us -> none  [shards(): lax.all_gather(dense_weight, 'req', axis=1, tiled=True)]
    all_gather x1, waiting for transfers between devices: 140 us -> 94.4 us  [shards(): lax.all_gather(fc2_weight, 'req', axis=1, tiled=True)]
    all_gather x1, waiting for transfers between devices: 135 us -> 92 us  [shards(): projected = add_rows(lax.all_gather(qkv_local, 'req', axis=0, tiled=True))]
    pmin x1, blocking collectives: 34.2 us -> 61.2 us  [shards(): starts = lax.pmin(earliest_rows, 'req')]
    all_to_all x0 -> x1, starting transfers between devices: none -> 18.9 us  [gather_over(): parts = lax.all_to_all(parts, name, split_axis=0, concat_axis=0)]
  transfers between devices with their start and end apart: 10 -> 10, of which waited for: 8 -> 7; matrix products, arithmetic and copies ran while one was open for 6% -> 8% of each run, Pallas kernels for 0% -> 0%
where the time goes in v1:
time: 545 us; the launch traced here: 544 us
  waiting for transfers between devices  372 us (68%)
  blocking collectives  61.2 us (11%)
  starting transfers between devices  40.1 us (7%)
  matrix products  23.1 us (4%)
  other arithmetic  18.1 us (3%)
  between operations  14.4 us (3%)
  local copies, waits for them, and re-layouts  13.2 us (2%)
    all_gather x1, waiting for transfers between devices, shards(): lifted = add_rows(lax.all_gather(fc1_weight, 'req', axis=0, tiled=True))  140 us
    all_gather x1, waiting for transfers between devices, shards(): lax.all_gather(fc2_weight, 'req', axis=1, tiled=True)  94.4 us
    all_gather x1, waiting for transfers between devices, shards(): projected = add_rows(lax.all_gather(qkv_local, 'req', axis=0, tiled=True))  92 us
    pmin x1, blocking collectives, shards(): starts = lax.pmin(earliest_rows, 'req')  61.2 us
    all_to_all x1, waiting for transfers between devices, shards(): lax.all_to_all(outgoing.reshape(req_count, page_cap, PAGE * 2 * head_cols...  22.2 us
    all_to_all x1, starting transfers between devices, gather_over(): parts = lax.all_to_all(parts, name, split_axis=0, concat_axis=0)  18.9 us
    all_to_all x1, waiting for transfers between devices, shards(): lax.all_to_all(filled.reshape(req_count, page_cap), 'req', split_axis=0,...  12.6 us
  transfers between devices with their start and end apart: 10, of which 7 were waited for; matrix products, arithmetic and copies ran while one was open for 8% of the time, Pallas kernels for 0%

profile of v1, /device:TPU:2, one launch (start us, length us, event | category | flops | bytes accessed | tf_op | source)
XLA Modules:
  0.0 544.5 jit_solution(3886715307231017203)
XLA Ops:
  10.2 1.8 stack.5
  12.0 18.9 %all-to-all-start = ((bf16[64,256,32]{1,2,0:T(8,128)(2,1)}), bf16[64,256,32]{1,2,0:T(8,128)(2,1)S(1)}, u32[]{:S(2)}, u32[]{:S(2)}) async-start(bf16[64,256,32]{1,2,0:T(8,128)(2,1)} %stack.5), calls=%async_computation | async-start | bytes 2097152 | tf_op jit(solution)/shard_map/all_to_all | solution.py:18
  31.7 61.2 %pmin.7 = s32[43]{0:T(128)S(1)} all-reduce(s32[43]{0:T(128)S(1)} %select_reduce_fusion.6), channel_id=1, replica_groups=mesh['req'=64,'tensor'=8] {'req'}, use_global_device_ids=true, to_apply=%region_3.4 | all-reduce | flops 43 | bytes 344 | tf_op jit(solution)/shard_map/pmin | solution.py:134
  95.3 1.9 constant_dynamic-update-slice_fusion.8
  97.3 1.9 constant_dynamic-update-slice_fusion.4
  103.1 92.0 %all-gather.7.cloned.1.call-done = bf16[2048,768]{1,0:T(8,128)(2,1)} async-done(((bf16[32,768]{1,0:T(8,128)(2,1)}), bf16[2048,768]{1,0:T(8,128)(2,1)}) %all-gather.7.cloned.1.call-update) | async-done | bytes 3145744 | tf_op jit(solution)/shard_map/all_gather | solution.py:140
  195.1 4.0 convolution_add_fusion.1
  200.7 1.9 collective-permute-start
  202.6 4.1 collective-permute-start.1
  206.7 1.9 constant_dynamic-update-slice_fusion
  208.7 3.0 collective-permute-done
  211.7 5.8 %collective-permute-done.1 = bf16[512,2,256]{0,2,1:T(8,128)(2,1)S(1)} collective-permute-done((bf16[512,2,256]{0,2,1:T(8,128)(2,1)S(1)}, bf16[512,2,256]{0,2,1:T(8,128)(2,1)S(1)}, u32[]{:S(2)}, u32[]{:S(2)}) %collective-permute-start.1) | collective-permute-done | bytes 524320 | tf_op jit(solution)/shard_map/ppermute | solution.py:25
  218.6 19.6 %while.11 = (s32[]{:T(128)}, bf16[4,256,64]{1,2,0:T(8,128)(2,1)S(1)}, s32[4]{0:T(128)S(1)}, bf16[256,256]{0,1:T(8,128)(2,1)S(1)}, bf16[1536,256]{0,1:T(8,128)(2,...) while((s32[]{:T(128)}, ...), condition=%wide.region_25.26_spmd.clone, body=%wide.region_22.25_spmd.clone.sunk | while | flops 112492032 | bytes 5240527 | solution.py:95
  219.8 1.8 fusion.74
  229.6 1.8 fusion.74
  234.5 1.8 fusion.74
  238.2 1.8 fusion.59
  240.0 94.4 %all-gather.11.cloned.1.call-done = bf16[512,2048]{0,1:T(8,128)(2,1)} async-done(((bf16[512,32]{0,1:T(8,128)(2,1)}), bf16[512,2048]{0,1:T(8,128)(2,1)}) %all-gather.11.cloned.1.call-update) | async-done | bytes 2097168 | tf_op jit(solution)/shard_map/all_gather | solution.py:218
  334.5 139.8 %all-gather.9.cloned.1.call-done = bf16[2048,512]{1,0:T(8,128)(2,1)} async-done(((bf16[32,512]{1,0:T(8,128)(2,1)}), bf16[2048,512]{1,0:T(8,128)(2,1)}) %all-gather.9.cloned.1.call-update) | async-done | bytes 2097168 | tf_op jit(solution)/shard_map/all_gather | solution.py:141
  474.3 5.7 %convolution_add_fusion = f32[256,2048]{1,0:T(8,128)} fusion(f32[256,2048]{1,0:T(8,128)} %fusion.59, bf16[512,2048]{0,1:T(8,128)(2,1)} %all-gather.11.cloned.1.call-done, bf16[2048,512]{1,0:T(8,128)(2,1)} %all-gather.9.cloned.1.call-done, f32[512]{0:T(512)S(1)} %copy-done.23, bf16[256,2048]{1,0:T(8,128)(2,1)S(1)} %copy-done, f32[2048]{0:T(1024)S(1)} %copy-done.20, ...), kind=kOutput, calls=%fused_computation.21 | convolution fusion | flops 1078722560 | bytes 9457664 | tf_op jit(solution)/shard_map/dot_general | solution.py:216
  481.9 10.3 %all-to-all-start.1 = ((bf16[64,1,2]{2,1,0:T(2,128)(2,1)}), bf16[64,1,2]{2,1,0:T(2,128)(2,1)S(1)}, u32[]{:S(2)}, u32[]{:S(2)}) async-start(bf16[64,1,2]{2,1,0:T(2,128)(2,1)} %all_to_all.16), calls=%async_computation.2 | async-start | bytes 65536 | tf_op jit(solution)/shard_map/all_to_all | solution.py:174
  494.2 12.6 %all-to-all-done.1 = bf16[64,1,2]{2,1,0:T(2,128)(2,1)S(1)} async-done(((bf16[64,1,2]{2,1,0:T(2,128)(2,1)}), bf16[64,1,2]{2,1,0:T(2,128)(2,1)S(1)}, u32[]{:S(2)}, u32[]{:S(2)}) %all-to-all-start.1) | async-done | bytes 288 | tf_op jit(solution)/shard_map/all_to_all | solution.py:174
  506.8 4.8 all-to-all-start.2
  512.5 22.2 %all-to-all-done.2 = bf16[64,2,2048]{2,1,0:T(2,128)(2,1)S(1)} async-done(((bf16[64,2,2048]{2,1,0:T(2,128)(2,1)}), bf16[64,2,2048]{2,1,0:T(2,128)(2,1)S(1)}, u32[]{:S(2)}, u32[]{:S(2)}) %all-to-all-start.2) | async-done | bytes 524320 | tf_op jit(solution)/shard_map/all_to_all | solution.py:167
  (137 shorter events, 31.9 us)
Async XLA Ops:
  7.2 92.3 %copy-start.8 = (f32[3,256]{1,0:T(4,128)S(1)}, f32[3,256]{1,0:T(4,128)}, u32[]{:S(2)}) copy-start(f32[3,256]{1,0:T(4,128)} %param.27) | copy-start | bytes 9220
  7.2 92.3 %copy-start.3 = (bf16[256,2,256]{2,1,0:T(2,128)(2,1)S(1)}, bf16[256,2,256]{2,1,0:T(2,128)(2,1)}, u32[]{:S(2)}) copy-start(bf16[256,2,256]{2,1,0:T(2,128)(2,1)} %param.34) | copy-start | bytes 786436
  7.2 92.7 %all-gather.5.cloned.1.call-start = ((), (), s32[]{:S(2)}) async-start(), calls=%async_computation.4 | async-start | bytes 1179648 | tf_op jit(solution)/shard_map/all_gather | solution.py:125
  7.9 187.1 %all-gather.7.cloned.1.call-start = ((), (), s32[]{:S(2)}) async-start(), calls=%async_computation.5 | async-start | bytes 3194880 | tf_op jit(solution)/shard_map/all_gather | solution.py:140
  9.4 325.0 %all-gather.11.cloned.1.call-start = ((), (), s32[]{:S(2)}) async-start(), calls=%async_computation.7 | async-start | bytes 2129920 | tf_op jit(solution)/shard_map/all_gather | solution.py:218
  12.0 183.1 %copy-start.19 = (f32[2048]{0:T(1024)S(1)}, f32[2048]{0:T(1024)}, u32[]{:S(2)}) copy-start(f32[2048]{0:T(1024)} %param.25) | copy-start | bytes 24580
  12.0 183.1 %copy-start.21 = (f32[2048]{0:T(1024)S(1)}, f32[2048]{0:T(1024)}, u32[]{:S(2)}) copy-start(f32[2048]{0:T(1024)} %param.24) | copy-start | bytes 24580
  12.0 226.2 %all-to-all-start = ((bf16[64,256,32]{1,2,0:T(8,128)(2,1)}), bf16[64,256,32]{1,2,0:T(8,128)(2,1)S(1)}, u32[]{:S(2)}, u32[]{:S(2)}) async-start(bf16[64,256,32]{1,2,0:T(8,128)(2,1)} %stack.5), calls=%async_computation | async-start | bytes 2097152 | tf_op jit(solution)/shard_map/all_to_all | solution.py:18
  30.9 443.4 %all-gather.9.cloned.1.call-start = ((), (), s32[]{:S(2)}) async-start(), calls=%async_computation.6 | async-start | bytes 2129920 | tf_op jit(solution)/shard_map/all_gather | solution.py:141
  31.4 504.9 %reduce-scatter.2.cloned.1.call-start = ((), (), s32[]{:S(2)}) async-start(), calls=%async_computation.8 | async-start | bytes 2359296 | tf_op jit(solution)/shard_map/reduce_scatter | solution.py:222
  95.3 99.8 %copy-start.4 = (s32[256]{0:T(256)}, s32[256]{0:T(256)S(1)}, u32[]{:S(2)}) copy-start(s32[256]{0:T(256)S(1)} %get-tuple-element.253) | copy-start | bytes 3076
  99.4 95.7 %copy-start.6 = (s32[256]{0:T(256)}, s32[256]{0:T(256)S(1)}, u32[]{:S(2)}) copy-start(s32[256]{0:T(256)S(1)} %get-tuple-element.256) | copy-start | bytes 3076
  99.9 95.2 %copy-start = (bf16[256,2048]{1,0:T(8,128)(2,1)S(1)}, bf16[256,2048]{1,0:T(8,128)(2,1)}, u32[]{:S(2)}) copy-start(bf16[256,2048]{1,0:T(8,128)(2,1)} %all-gather.5.cloned.1.call-done) | copy-start | bytes 3145732
  101.4 97.6 %copy-start.9 = (f32[256]{0:T(256)}, f32[256]{0:T(256)S(1)}, u32[]{:S(2)}) copy-start(f32[256]{0:T(256)S(1)} %broadcast_multiply_fusion) | copy-start | bytes 3076
  103.1 96.0 %copy-start.16 = (f32[256]{0:T(256)}, f32[256]{0:T(256)S(1)}, u32[]{:S(2)}) copy-start(f32[256]{0:T(256)S(1)} %add_rsqrt_fusion) | copy-start | bytes 3076
  200.7 11.0 %collective-permute-start = (bf16[512,2,256]{0,2,1:T(8,128)(2,1)S(1)}, bf16[512,2,256]{0,2,1:T(8,128)(2,1)S(1)}, u32[]{:S(2)}, u32[]{:S(2)}) collective-permute-start(bf16[512,2,256]{0,2,1:T(8,128)(2,1)S(1)} %pad_maximum_fusion.1), channel_id=1, source_target_pairs={{0,8},{8,16},{16,24},{24,32},{32,40},{40,48},{48,56},{56,64},{64,7... | collective-permute-start | bytes 1572872 | tf_op jit(solution)/shard_map/ppermute | solution.py:25
  202.6 14.9 %collective-permute-start.1 = (bf16[512,2,256]{0,2,1:T(8,128)(2,1)S(1)}, bf16[512,2,256]{0,2,1:T(8,128)(2,1)S(1)}, u32[]{:S(2)}, u32[]{:S(2)}) collective-permute-start(bf16[512,2,256]{0,2,1:T(8,128)(2,1)S(1)} %pad_maximum_fusion.1), channel_id=1, source_target_pairs={{0,16},{8,24},{16,32},{24,40},{32,48},{40,56},{48,64},{56,72},{64,... | collective-permute-start | bytes 1572872 | tf_op jit(solution)/shard_map/ppermute | solution.py:25
  238.1 236.1 %copy-start.10 = (f32[256]{0:T(256)S(1)}, f32[256]{0:T(256)}, u32[]{:S(2)}) copy-start(f32[256]{0:T(256)} %copy-done.9) | copy-start | bytes 3076
  238.1 236.1 %copy-start.17 = (f32[256]{0:T(256)S(1)}, f32[256]{0:T(256)}, u32[]{:S(2)}) copy-start(f32[256]{0:T(256)} %copy-done.16) | copy-start | bytes 3076
  238.2 236.1 %copy-start.20 = (f32[2048]{0:T(1024)S(1)}, f32[2048]{0:T(1024)}, u32[]{:S(2)}) copy-start(f32[2048]{0:T(1024)} %param.25) | copy-start | bytes 24580
  238.2 236.1 %copy-start.22 = (f32[2048]{0:T(1024)S(1)}, f32[2048]{0:T(1024)}, u32[]{:S(2)}) copy-start(f32[2048]{0:T(1024)} %param.24) | copy-start | bytes 24580
  238.2 236.1 %copy-start.23 = (f32[512]{0:T(512)S(1)}, f32[512]{0:T(512)}, u32[]{:S(2)}) copy-start(f32[512]{0:T(512)} %param.31) | copy-start | bytes 6148
  481.9 24.9 %all-to-all-start.1 = ((bf16[64,1,2]{2,1,0:T(2,128)(2,1)}), bf16[64,1,2]{2,1,0:T(2,128)(2,1)S(1)}, u32[]{:S(2)}, u32[]{:S(2)}) async-start(bf16[64,1,2]{2,1,0:T(2,128)(2,1)} %all_to_all.16), calls=%async_computation.2 | async-start | bytes 65536 | tf_op jit(solution)/shard_map/all_to_all | solution.py:174
  506.8 27.8 %all-to-all-start.2 = ((bf16[64,2,2048]{2,1,0:T(2,128)(2,1)}), bf16[64,2,2048]{2,1,0:T(2,128)(2,1)S(1)}, u32[]{:S(2)}, u32[]{:S(2)}) async-start(bf16[64,2,2048]{2,1,0:T(2,128)(2,1)} %reshape.264), calls=%async_computation.3 | async-start | bytes 1048576 | tf_op jit(solution)/shard_map/all_to_all | solution.py:167
  (10 other events, 225.5 us)
Sparse Core Ops, SparseCore 0:
  10.2 34.8 all-gather.4
  48.6 146.4 all-gather.6
  198.0 136.3 all-gather.10
  337.3 136.9 all-gather.8
  480.1 34.3 reduce-scatter.1
